TPU v7x, 32 devices: a whole 2x2x4 slice. The times are simulated.
32 devices in a mesh: section: 2 (over y), expert: 8 (over z, x), dp: 2 (over core).
Axes of the slice: x: 2, y: 2, z: 4, core: 2. Of those that a mesh axis runs over, the one named last changes fastest.
Arguments:
- tokens_in: bfloat16 [8, 256, 2048], P(None, ('expert', 'dp')), may hold values from -6 to 6
- cotangent: bfloat16 [8, 256, 2048], P(None, ('expert', 'dp')), may hold values from -4 to 4
- routes: int32 [2, 8, 256, 8], P('section', None, ('expert', 'dp')), may hold values from 0 to 15, all different within a row; in each aligned block of 16 rows (0 to 15, 16 to 31, ..., all dimensions but the last counted through in order) at most 10 rows name the same one
- router_weights: float32 [2, 8, 256, 8], P('section', None, ('expert', 'dp')), may hold values from 0.1 to 0.6
- norm_gain: float32 [2, 2048], P('section'), may hold values from 0.25 to 1.75
- w_gate: bfloat16 [2, 16, 2048, 512], P('section', 'expert'), may hold values from -0.125 to 0.125
- w_up: bfloat16 [2, 16, 2048, 512], P('section', 'expert'), may hold values from -0.125 to 0.125
- w_down: bfloat16 [2, 16, 512, 2048], P('section', 'expert'), may hold values from -0.25 to 0.25
Outputs:
- layer_out: bfloat16 [2, 8, 256, 2048], P('section', None, ('expert', 'dp'))
- input_grad: bfloat16 [2, 8, 256, 2048], P('section', None, ('expert', 'dp'))
- grad_gate: bfloat16 [2, 16, 2048, 512], P('section', 'expert', 'dp')
- grad_up: bfloat16 [2, 16, 2048, 512], P('section', 'expert', 'dp')
- grad_down: bfloat16 [2, 16, 512, 2048], P('section', 'expert', 'dp')
Inputs may be any that keep to these rules, and one draw needn't show every extreme that they name: `routes`: each row names 8 different experts. In each aligned block of 16 rows (the tokens of one device for one layer and one micro-batch) no expert is named by more than 10 rows, and in some blocks one is named by exactly 10.
All inputs are finite; a program needn't handle non-finite values.
Results may differ from a plain program's by a relative error of at most 0.022.
Values may be sent and summed in bfloat16 or wider, within the bound.
A program may use at most 128 MiB of HBM per device.

v0:
```python
import jax
import jax.numpy as jnp
from jax import lax
from jax.sharding import PartitionSpec as P

epsilon = 1e-06
ROW_LIMIT = 1024


def from_behind(block, axis, distance):
    devices = range(lax.axis_size(axis))
    route = [(i - distance, i) for i in devices if i - distance in devices]
    return lax.ppermute(block, axis, route)


def pick(section_id, by_section):
    entries = list(by_section.items())
    chosen = entries[0][1]
    for section, value in entries[1:]:
        if value is not chosen:
            chosen = jnp.where(section_id == section, value, chosen)
    return chosen


def weight_table(route_ids, route_weights, experts, expert_count):
    labels = jnp.arange(experts, dtype=jnp.int32)[:, None, None, None]
    dense = jnp.sum(jnp.where(route_ids[None] == labels, route_weights[None], 0.0), axis=3)
    dense = dense.reshape((expert_count, experts // expert_count) + dense.shape[1:])
    return lax.all_to_all(dense, "expert", split_axis=0, concat_axis=0, tiled=True)


def on_device(tokens_in, cotangent, routes, router_weights, norm_gain, w_gate, w_up, w_down):
    micro_count, token_rows, width = tokens_in.shape
    held, hidden_units = (w_gate.shape[1], w_gate.shape[3])
    sections = lax.axis_size("section")
    expert_count = lax.axis_size("expert")
    dp_count = lax.axis_size("dp")
    chunks = 1
    while (
        micro_count % (2 * chunks) == 0
        and micro_count * token_rows * expert_count > ROW_LIMIT * chunks
    ):
        chunks *= 2
    per_chunk = micro_count // chunks
    own_rows = per_chunk * token_rows
    ticks = sections + chunks - 1
    inner = held * hidden_units
    section_id = lax.axis_index("section")
    gain_row = norm_gain[0]
    table = weight_table(routes[0], router_weights[0], held * expert_count, expert_count)
    w_in = jnp.concatenate(
        [w_gate[0, e] for e in range(held)] + [w_up[0, e] for e in range(held)], axis=1
    )
    w_out = w_down[0].reshape(inner, width)

    def chunk_of(array, chunk, axis):
        if chunks == 1:
            return array
        return lax.dynamic_slice_in_dim(array, chunk * per_chunk, per_chunk, axis)

    def spread_weights(chunk):
        rows = chunk_of(table, chunk, 2).transpose(0, 2, 3, 1).reshape(-1, held)
        return jnp.repeat(rows, hidden_units, axis=1)

    def gather(rows):
        return lax.all_gather(rows, "expert", axis=0, tiled=True)

    def scatter(rows):
        return lax.psum_scatter(rows, "expert", scatter_dimension=0, tiled=True)

    def rms(hidden):
        widened = hidden.astype(jnp.float32)
        return (widened, lax.rsqrt(jnp.mean(widened * widened, axis=-1, keepdims=True) + epsilon))

    compact = sections > 2

    def keep(store, value, owner):
        if not compact:
            store.append(value)
        elif not store:
            store.extend([value] * chunks)
        else:
            store[:] = [
                jnp.where(section_id == owner(c), value, old) for c, old in enumerate(store)
            ]
            store[:] = lax.optimization_barrier(store)

    def at(store, chunk, shift):
        return store[chunk] if compact else store[chunk + shift]

    hiddens, rows_in, pre_acts, acts, outputs = ([], [], [], [], [])
    incoming = None
    for tick in range(ticks):
        chunk = jnp.clip(tick - section_id, 0, chunks - 1)
        hidden = None
        if tick < chunks:
            hidden = chunk_of(tokens_in, chunk, 0).reshape(own_rows, width)
        if tick > 0:
            hidden = incoming if hidden is None else jnp.where(section_id == 0, hidden, incoming)
        widened, inv_rms = rms(hidden)
        gathered = gather((widened * inv_rms * gain_row).astype(jnp.bfloat16))
        pre = jnp.dot(gathered, w_in, preferred_element_type=jnp.float32).astype(jnp.bfloat16)
        gate, up = (pre[:, :inner].astype(jnp.float32), pre[:, inner:].astype(jnp.float32))
        act = (gate * jax.nn.sigmoid(gate) * up * spread_weights(chunk)).astype(jnp.bfloat16)
        mixed = jnp.dot(act, w_out, preferred_element_type=jnp.float32).astype(jnp.bfloat16)
        output = (widened + scatter(mixed).astype(jnp.float32)).astype(jnp.bfloat16)
        if tick < ticks - 1:
            incoming = from_behind(output, "section", 1)
        keep(hiddens, hidden, lambda c: tick - c)
        keep(rows_in, gathered, lambda c: tick - c)
        keep(pre_acts, pre, lambda c: tick - c)
        keep(acts, act, lambda c: tick - c)
        keep(outputs, output, lambda c: tick - c)
    grads_in, pre_grads, results = ([], [], [])
    for tick in range(ticks):
        chunk = jnp.clip(tick - (sections - 1 - section_id), 0, chunks - 1)
        active = {
            s: tick - (sections - 1 - s)
            for s in range(sections)
            if 0 <= tick - (sections - 1 - s) < chunks
        }
        grad_out = None
        if tick < chunks:
            grad_out = chunk_of(cotangent, chunk, 0).reshape(own_rows, width)
        if tick > 0:
            grad_out = (
                incoming
                if grad_out is None
                else jnp.where(section_id == sections - 1, grad_out, incoming)
            )
        gathered = gather(grad_out)
        pre = pick(section_id, {s: at(pre_acts, c, s) for s, c in active.items()})
        gate, up = (pre[:, :inner].astype(jnp.float32), pre[:, inner:].astype(jnp.float32))
        act_grad = lax.dot_general(
            gathered, w_out, (((1,), (1,)), ((), ())), preferred_element_type=jnp.float32
        )
        act_grad = act_grad * spread_weights(chunk)
        sig = jax.nn.sigmoid(gate)
        pre_grad = jnp.concatenate(
            [
                (act_grad * up * sig * (1.0 + gate * (1.0 - sig))).astype(jnp.bfloat16),
                (act_grad * gate * sig).astype(jnp.bfloat16),
            ],
            axis=1,
        )
        row_grad = lax.dot_general(
            pre_grad, w_in, (((1,), (1,)), ((), ())), preferred_element_type=jnp.float32
        ).astype(jnp.bfloat16)
        dnormed = scatter(row_grad).astype(jnp.float32)
        hidden = pick(section_id, {s: at(hiddens, c, s) for s, c in active.items()})
        widened, inv_rms = rms(hidden)
        unit = widened * inv_rms
        scaled = dnormed * gain_row
        result = (
            grad_out.astype(jnp.float32)
            + inv_rms * (scaled - unit * jnp.mean(scaled * unit, axis=-1, keepdims=True))
        ).astype(jnp.bfloat16)
        if tick < ticks - 1:
            incoming = from_behind(result, "section", -1)
        keep(grads_in, gathered, lambda c: sections - 1 - tick + c)
        keep(pre_grads, pre_grad, lambda c: sections - 1 - tick + c)
        keep(results, result, lambda c: sections - 1 - tick + c)

    def contract(left, right):
        return lax.dot_general(
            left, right, (((0,), (0,)), ((), ())), preferred_element_type=jnp.float32
        )

    def summed(pairs):
        total = contract(*pairs[0])
        for pair in pairs[1:]:
            total = total + contract(*pair)
        return total.astype(jnp.bfloat16)

    def split_columns(array, groups, part):
        size = array.shape[1] // groups
        piece = size // dp_count
        cuts = [
            lax.dynamic_slice_in_dim(array, g * size + part * piece, piece, 1)
            for g in range(groups)
        ]
        return cuts[0] if groups == 1 else jnp.concatenate(cuts, axis=1)

    def in_weight_part(part):

        def branch(section):
            back = sections - 1 - section
            return lambda: summed(
                [
                    (split_columns(at(rows_in, c, section), 1, part), at(pre_grads, c, back))
                    for c in range(chunks)
                ]
            )

        if compact:
            return branch(0)()
        return lax.switch(section_id, [branch(s) for s in range(sections)])

    def out_weight_part(part):

        def branch(section):
            back = sections - 1 - section
            return lambda: summed(
                [
                    (split_columns(at(acts, c, section), held, part), at(grads_in, c, back))
                    for c in range(chunks)
                ]
            )

        if compact:
            return branch(0)()
        return lax.switch(section_id, [branch(s) for s in range(sections)])

    dp_id = lax.axis_index("dp")

    def over_dp(part_fn):
        total = part_fn(dp_id).astype(jnp.float32)
        for distance in range(1, dp_count):
            ring = [(i, (i + distance) % dp_count) for i in range(dp_count)]
            other = part_fn((dp_id + distance) % dp_count)
            total = total + lax.ppermute(other, "dp", ring).astype(jnp.float32)
        return total.astype(jnp.bfloat16)

    out_grads = over_dp(out_weight_part)
    in_grads = over_dp(in_weight_part)
    grad_gate = jnp.stack(
        [in_grads[:, e * hidden_units : (e + 1) * hidden_units] for e in range(held)]
    )
    grad_up = jnp.stack(
        [
            in_grads[:, inner + e * hidden_units : inner + (e + 1) * hidden_units]
            for e in range(held)
        ]
    )
    grad_down = out_grads.reshape(held, hidden_units // dp_count, width)

    def in_order(per_tick, first_tick):
        kept = pick(
            section_id,
            {
                s: jnp.concatenate([at(per_tick, c, first_tick(s)) for c in range(chunks)], axis=0)
                for s in range(sections)
            },
        )
        return kept.reshape(1, micro_count, token_rows, width)

    layer_out = in_order(outputs, lambda s: s)
    input_grad = in_order(results, lambda s: sections - 1 - s)
    return (layer_out, input_grad, grad_gate[None], grad_up[None], grad_down[None])


def solution(mesh):
    placed = (
        P(None, ("expert", "dp"), None),
        P(None, ("expert", "dp"), None),
        P("section", None, ("expert", "dp"), None),
        P("section", None, ("expert", "dp"), None),
        P("section", None),
        P("section", "expert", None, None),
        P("section", "expert", None, None),
        P("section", "expert", None, None),
    )
    return jax.shard_map(
        on_device,
        mesh=mesh,
        in_specs=placed,
        out_specs=(
            P("section", None, ("expert", "dp"), None),
            P("section", None, ("expert", "dp"), None),
            P("section", "expert", "dp", None),
            P("section", "expert", "dp", None),
            P("section", "expert", "dp", None),
        ),
        check_vma=False,
    )
```

profile of v0, /device:TPU:0, one launch (start us, length us, event | category | flops | bytes accessed | tf_op | source)
XLA Modules:
  0.0 759.2 jit_solution(15389432934267854801)
XLA Ops:
  7.2 1.2 fusion.72
  8.5 2.0 fusion.66
  10.6 1.0 select_reduce_fusion
  11.6 0.7 reshape.77
  12.2 7.3 all-to-all-start
  19.6 6.5 slice_bitcast_fusion.1
  26.1 0.6 broadcast.69
  26.7 0.7 reduce.1
  27.5 0.4 copy.33
  28.0 1.4 broadcast_in_dim.36
  29.4 3.0 copy.35
  32.4 53.9 %all-gather.5.cloned.1.call-done = bf16[1024,2048]{1,0:T(8,128)(2,1)} async-done(((bf16[128,2048]{1,0:T(8,128)(2,1)}), bf16[1024,2048]{1,0:T(8,128)(2,1)}) %all-gather.5.cloned.1.call-update) | async-done | bytes 4194320 | tf_op jit(solution)/shard_map/all_gather | solution.py:66
  86.3 13.0 %convolution_convert_fusion.5 = bf16[1024,2048]{1,0:T(8,128)(2,1)S(1)} fusion(bf16[1024,2048]{1,0:T(8,128)(2,1)} %all-gather.5.cloned.1.call-done, bf16[2048,512]{1,0:T(8,128)(2,1)} %get-tuple-element.115, bf16[2048,512]{1,0:T(8,128)(2,1)S(1)} %get-tuple-element.114, bf16[2048,512]{1,0:T(8,128)(2,1)} %get-tuple-element.116, ...), kind=kOutput, calls=%fused_computation.84 | convolution fusion | flops 8625586176 | bytes 16777216 | tf_op jit(solution)/shard_map/dot_general | solution.py:102
  99.3 1.5 fusion.31
  100.9 0.6 copy-done.4
  101.4 1.6 copy-done.22
  103.0 6.2 convolution_convert_fusion.7
  109.3 87.0 %reduce-scatter.5.cloned.1.call-done = bf16[128,2048]{1,0:T(8,128)(2,1)} async-done(((bf16[1024,2048]{1,0:T(8,128)(2,1)}), bf16[128,2048]{1,0:T(8,128)(2,1)}) %reduce-scatter.5.cloned.1.call-update) | async-done | bytes 524304 | tf_op jit(solution)/shard_map/reduce_scatter | solution.py:69
  196.2 1.2 fusion.73
  197.4 3.4 collective-permute-start
  200.8 10.8 %collective-permute-done = bf16[128,2048]{1,0:T(8,128)(2,1)S(1)} collective-permute-done((bf16[128,2048]{1,0:T(8,128)(2,1)S(1)}, bf16[128,2048]{1,0:T(8,128)(2,1)S(1)}, u32[]{:S(2)}, u32[]{:S(2)}) %collective-permute-start) | collective-permute-done | bytes 524320 | tf_op jit(solution)/shard_map/ppermute | solution.py:13
  211.8 1.0 fusion.55
  212.8 0.5 all-gather.9.cloned.1.call-update
  213.6 73.3 %all-gather.7.cloned.1.call-done = bf16[1024,2048]{1,0:T(8,128)(2,1)} async-done(((bf16[128,2048]{1,0:T(8,128)(2,1)}), bf16[1024,2048]{1,0:T(8,128)(2,1)}) %all-gather.7.cloned.1.call-update) | async-done | bytes 4194320 | tf_op jit(solution)/shard_map/all_gather | solution.py:66
  286.9 14.3 %convolution_convert_fusion.4 = bf16[1024,2048]{1,0:T(8,128)(2,1)} fusion(bf16[1024,2048]{1,0:T(8,128)(2,1)} %all-gather.7.cloned.1.call-done, bf16[2048,512]{1,0:T(8,128)(2,1)} %get-tuple-element.115, bf16[2048,512]{1,0:T(8,128)(2,1)} %copy-done.18, bf16[2048,512]{1,0:T(8,128)(2,1)} %get-tuple-element.116, bf16[2048,512]{1,0:T(8,128)(2,1)} %get-tuple-element.117), kind=kOutput, calls=%fused_computation.83 | convolution fusion | flops 8625586176 | bytes 16777216 | tf_op jit(solution)/shard_map/dot_general | solution.py:102
  301.2 59.1 %all-gather.9.cloned.1.call-done = bf16[1024,2048]{1,0:T(8,128)(2,1)} async-done(((bf16[128,2048]{1,0:T(8,128)(2,1)}), bf16[1024,2048]{1,0:T(8,128)(2,1)}) %all-gather.9.cloned.1.call-update) | async-done | bytes 4194320 | tf_op jit(solution)/shard_map/all_gather | solution.py:66
  360.3 12.3 %fusion.39 = (bf16[1024,1024]{1,0:T(8,128)(2,1)S(1)}, bf16[1024,1024]{1,0:T(8,128)(2,1)S(1)}, bf16[1024,1024]{1,0:T(8,128)(2,1)}) fusion(bf16[1024,2048]{1,0:T(8,128)(2,1)} %convolution_convert_fusion.4, f32[1024,1024]{1,0:T(8,128)} %bitcast.77, bf16[1024,2048]{1,0:T(8,128)(2,1)} %all-gather.9.cloned.1.call-done, bf16[1024,2048]{1,0:T(8,128)(2,1)} %bitcast.96), kind=kOutput, calls=%fused_computation.65 | convolution fusion | flops 4315938816 | bytes 23068672 | tf_op jit(solution)/shard_map/dot_general | solution.py:134
  372.6 1.3 copy-done.10
  373.9 0.7 copy-done.11
  374.6 12.6 %convolution_convert_fusion.3 = bf16[1024,2048]{1,0:T(8,128)(2,1)} fusion(bf16[1024,1024]{1,0:T(8,128)(2,1)S(1)} %get-tuple-element.106, bf16[1024,1024]{1,0:T(8,128)(2,1)S(1)} %get-tuple-element.105, bf16[2048,512]{1,0:T(8,128)(2,1)} %get-tuple-element.115, bf16[2048,512]{1,0:T(8,128)(2,1)} %copy-done.18, bf16[2048,512]{1,0:T(8,128)(2,1)} %get-tuple-element.116, ...), kind=kOutput, calls=%fused_computation.82 | convolution fusion | flops 8633974784 | bytes 16777216 | tf_op jit(solution)/shard_map/dot_general | solution.py:146
  387.3 86.9 %reduce-scatter.9.cloned.1.call-done = bf16[128,2048]{1,0:T(8,128)(2,1)} async-done(((bf16[1024,2048]{1,0:T(8,128)(2,1)}), bf16[128,2048]{1,0:T(8,128)(2,1)}) %reduce-scatter.9.cloned.1.call-update) | async-done | bytes 524304 | tf_op jit(solution)/shard_map/reduce_scatter | solution.py:69
  474.2 1.4 fusion.56
  475.6 1.5 fusion.60
  477.1 0.8 copy-done.16
  477.9 1.3 collective-permute-start.1
  479.2 13.9 %collective-permute-done.1 = bf16[128,2048]{1,0:T(8,128)(2,1)S(1)} collective-permute-done((bf16[128,2048]{1,0:T(8,128)(2,1)S(1)}, bf16[128,2048]{1,0:T(8,128)(2,1)S(1)}, u32[]{:S(2)}, u32[]{:S(2)}) %collective-permute-start.1) | collective-permute-done | bytes 524320 | tf_op jit(solution)/shard_map/ppermute | solution.py:13
  493.0 0.8 copy-done.8
  494.4 9.4 %convolution_convert_fusion.6 = bf16[1024,2048]{1,0:T(8,128)(2,1)} fusion(bf16[1024,1024]{1,0:T(8,128)(2,1)} %get-tuple-element.111, bf16[1024,2048]{1,0:T(8,128)(2,1)} %bitcast.97), kind=kOutput, calls=%fused_computation.85 | convolution fusion | flops 4297064448 | bytes 10485760 | tf_op jit(solution)/shard_map/dot_general | solution.py:105
  503.8 62.4 %all-gather.11.cloned.1.call-done = bf16[1024,2048]{1,0:T(8,128)(2,1)} async-done(((bf16[128,2048]{1,0:T(8,128)(2,1)}), bf16[1024,2048]{1,0:T(8,128)(2,1)}) %all-gather.11.cloned.1.call-update) | async-done | bytes 4194320 | tf_op jit(solution)/shard_map/all_gather | solution.py:66
  566.1 11.9 %fusion.34 = (bf16[1024,1024]{1,0:T(8,128)(2,1)S(1)}, bf16[1024,1024]{1,0:T(8,128)(2,1)S(1)}) fusion(bf16[1024,2048]{1,0:T(8,128)(2,1)} %copy-done.4, f32[1024,1024]{1,0:T(8,128)} %bitcast.78, bf16[1024,2048]{1,0:T(8,128)(2,1)} %all-gather.11.cloned.1.call-done, bf16[1024,2048]{1,0:T(8,128)(2,1)} %bitcast.98), kind=kOutput, calls=%fused_computation.60 | convolution fusion | flops 4311744512 | bytes 20971520 | tf_op jit(solution)/shard_map/dot_general | solution.py:134
  578.0 1.3 copy-done.12
  579.3 0.7 copy-done.14
  580.0 12.7 %convolution_convert_fusion.2 = bf16[1024,2048]{1,0:T(8,128)(2,1)} fusion(bf16[1024,1024]{1,0:T(8,128)(2,1)S(1)} %get-tuple-element.104, bf16[1024,1024]{1,0:T(8,128)(2,1)S(1)} %get-tuple-element.103, bf16[2048,512]{1,0:T(8,128)(2,1)} %get-tuple-element.115, bf16[2048,512]{1,0:T(8,128)(2,1)} %copy-done.18, bf16[2048,512]{1,0:T(8,128)(2,1)} %get-tuple-element.116, ...), kind=kOutput, calls=%fused_computation.81 | convolution fusion | flops 8633974784 | bytes 16777216 | tf_op jit(solution)/shard_map/dot_general | solution.py:146
  592.8 5.1 pad_maximum_fusion.1
  597.9 2.4 pad_maximum_fusion.2
  600.3 9.6 %conditional.13 = (bf16[1024,2048]{1,0:T(8,128)(2,1)}) conditional(s32[]{:T(128)} %clamp.2, (s32[]{:T(128)}, bf16[1024,2048]{1,0:T(8,128)(2,1)}, bf16[1024,2048]{1,0:T(8,128)(2,1)}) %tuple.44, (s32[]{:T(128)}, bf16[1024,2048]{1,0:T(8,128)(2,1)}, bf16[1024,2048]{1,0:T(8,128)(2,1)}) %tuple.45), branch_computations={%region_11.12_spmd, %region_12.13_spmd} | conditional | flops 4294967296 | bytes 10485818
  600.5 9.4 %fusion.4 = bf16[1024,2048]{1,0:T(8,128)(2,1)} fusion(bf16[1024,2048]{1,0:T(8,128)(2,1)} %get-tuple-element.74, bf16[1024,2048]{1,0:T(8,128)(2,1)} %get-tuple-element.72, s32[]{:T(128)S(6)} %select_n.46), kind=kOutput, calls=%fused_computation.6 | convolution fusion | flops 4294967296 | bytes 10485764 | tf_op jit(solution)/shard_map/cond/branch_0_fun/dot_general | solution.py:165
  609.9 6.3 conditional.15
  610.0 6.0 fusion.20
  616.2 0.6 collective-permute-start.3
  616.8 39.9 %reduce-scatter.7.cloned.1.call-done = bf16[128,2048]{1,0:T(8,128)(2,1)} async-done(((bf16[1024,2048]{1,0:T(8,128)(2,1)}), bf16[128,2048]{1,0:T(8,128)(2,1)}) %reduce-scatter.7.cloned.1.call-update) | async-done | bytes 524304 | tf_op jit(solution)/shard_map/reduce_scatter | solution.py:69
  656.7 2.1 fusion.75
  658.7 10.7 %conditional.12 = (f32[1024,2048]{1,0:T(8,128)}) conditional(s32[]{:T(128)} %clamp.2, (s32[]{:T(128)}, bf16[1024,2048]{1,0:T(8,128)(2,1)}, bf16[1024,2048]{1,0:T(8,128)(2,1)}) %tuple.42, (s32[]{:T(128)}, bf16[1024,2048]{1,0:T(8,128)(2,1)}, bf16[1024,2048]{1,0:T(8,128)(2,1)}) %tuple.43), branch_computations={%region_9.10_spmd, %region_10.11_spmd} | conditional | flops 4299161600 | bytes 14680122 | solution.py:197
  658.7 10.7 %convert_convert_fusion = f32[1024,2048]{1,0:T(8,128)} fusion(bf16[1024,2048]{1,0:T(8,128)(2,1)} %get-tuple-element.68, bf16[1024,2048]{1,0:T(8,128)(2,1)} %get-tuple-element.66, s32[]{:T(128)S(6)} %select_n.44), kind=kOutput, calls=%fused_computation | convolution fusion | flops 4299161600 | bytes 14680068 | tf_op jit(solution)/shard_map/cond/branch_0_fun/dot_general | solution.py:165
  669.4 7.0 conditional.14
  669.8 6.6 fusion.10
  676.4 5.1 add_convert_fusion.1
  681.6 1.0 copy-done.3
  682.6 3.8 add_convert_fusion
  686.8 1.5 maximum_bitcast_fusion
  688.3 1.5 maximum_bitcast_fusion.1
  689.8 58.4 %reduce-scatter.11.cloned.1.call-done = bf16[128,2048]{1,0:T(8,128)(2,1)} async-done(((bf16[1024,2048]{1,0:T(8,128)(2,1)}), bf16[128,2048]{1,0:T(8,128)(2,1)}) %reduce-scatter.11.cloned.1.call-update) | async-done | bytes 524304 | tf_op jit(solution)/shard_map/reduce_scatter | solution.py:69
  748.2 1.4 fusion.67
  749.6 2.3 fusion.74
  (66 shorter events, 2.3 us)
Async XLA Ops:
  7.2 79.1 %all-gather.5.cloned.1.call-start = ((), (), s32[]{:S(2)}) async-start(), calls=%async_computation.5 | async-start | bytes 4718592 | tf_op jit(solution)/shard_map/all_gather | solution.py:66
  8.5 2.1 copy-start.20
  12.2 13.9 %all-to-all-start = ((f32[8,1,256]{2,1,0:T(1,128)}), f32[8,1,256]{2,1,0:T(1,128)S(1)}, u32[]{:S(2)}, u32[]{:S(2)}) async-start(f32[8,1,256]{2,1,0:T(1,128)} %reshape.77), calls=%async_computation | async-start | bytes 16384 | tf_op jit(solution)/shard_map/all_to_all | solution.py:29
  19.5 176.7 %reduce-scatter.5.cloned.1.call-start = ((), (), s32[]{:S(2)}) async-start(), calls=%async_computation.6 | async-start | bytes 4718592 | tf_op jit(solution)/shard_map/reduce_scatter | solution.py:69
  26.1 60.2 %copy-start.18 = (bf16[2048,512]{1,0:T(8,128)(2,1)}, bf16[2048,512]{1,0:T(8,128)(2,1)S(1)}, u32[]{:S(2)}) copy-start(bf16[2048,512]{1,0:T(8,128)(2,1)S(1)} %get-tuple-element.114) | copy-start | bytes 6291460
  86.3 13.1 %copy-start = (f32[128,8,2,512]{3,1,2,0:T(8,128)S(1)}, f32[128,8,2,512]{3,1,2,0:T(8,128)}, u32[]{:S(2)}) copy-start(f32[128,8,2,512]{3,1,2,0:T(8,128)} %copy.35) | copy-start | bytes 12582916
  99.3 2.1 copy-start.4
  99.3 3.7 copy-start.22
  109.2 87.0 %copy-start.1 = (bf16[8,16,2048]{2,1,0:T(8,128)(2,1)S(1)}, bf16[8,16,2048]{2,1,0:T(8,128)(2,1)}, u32[]{:S(2)}) copy-start(bf16[8,16,2048]{2,1,0:T(8,128)(2,1)} %param.16) | copy-start | bytes 1572868
  109.2 102.6 %copy-start.19 = (f32[1,2048]{1,0:T(1,128)S(1)}, f32[1,2048]{1,0:T(1,128)}, u32[]{:S(2)}) copy-start(f32[1,2048]{1,0:T(1,128)} %param.20) | copy-start | bytes 24580
  109.2 177.7 %all-gather.7.cloned.1.call-start = ((), (), s32[]{:S(2)}) async-start(), calls=%async_computation.7 | async-start | bytes 4718592 | tf_op jit(solution)/shard_map/all_gather | solution.py:66
  197.4 14.2 %copy-start.5 = (bf16[128,2048]{1,0:T(8,128)(2,1)}, bf16[128,2048]{1,0:T(8,128)(2,1)S(1)}, u32[]{:S(2)}) copy-start(bf16[128,2048]{1,0:T(8,128)(2,1)S(1)} %fusion.73) | copy-start | bytes 1572868
  197.4 14.2 %collective-permute-start = (bf16[128,2048]{1,0:T(8,128)(2,1)S(1)}, bf16[128,2048]{1,0:T(8,128)(2,1)S(1)}, u32[]{:S(2)}, u32[]{:S(2)}) collective-permute-start(bf16[128,2048]{1,0:T(8,128)(2,1)S(1)} %fusion.73), channel_id=1, source_target_pairs={{0,16},{1,17},{2,18},{3,19},{4,20},{5,21},{6,22},{7,23},{8,24},{9,... | collective-permute-start | bytes 1572872 | tf_op jit(solution)/shard_map/ppermute | solution.py:13
  212.8 147.5 %all-gather.9.cloned.1.call-start = ((), (), s32[]{:S(2)}) async-start(), calls=%async_computation.9 | async-start | bytes 4718592 | tf_op jit(solution)/shard_map/all_gather | solution.py:66
  213.4 260.8 %reduce-scatter.9.cloned.1.call-start = ((), (), s32[]{:S(2)}) async-start(), calls=%async_computation.10 | async-start | bytes 4718592 | tf_op jit(solution)/shard_map/reduce_scatter | solution.py:69
  372.6 1.3 copy-start.10
  372.6 2.0 copy-start.11
  387.2 88.4 %copy-start.7 = (bf16[8,16,2048]{2,1,0:T(8,128)(2,1)S(1)}, bf16[8,16,2048]{2,1,0:T(8,128)(2,1)}, u32[]{:S(2)}) copy-start(bf16[8,16,2048]{2,1,0:T(8,128)(2,1)} %param.17) | copy-start | bytes 1572868
  387.2 178.9 %all-gather.11.cloned.1.call-start = ((), (), s32[]{:S(2)}) async-start(), calls=%async_computation.11 | async-start | bytes 4718592 | tf_op jit(solution)/shard_map/all_gather | solution.py:66
  477.0 0.8 copy-start.16
  477.9 15.2 %collective-permute-start.1 = (bf16[128,2048]{1,0:T(8,128)(2,1)S(1)}, bf16[128,2048]{1,0:T(8,128)(2,1)S(1)}, u32[]{:S(2)}, u32[]{:S(2)}) collective-permute-start(bf16[128,2048]{1,0:T(8,128)(2,1)S(1)} %fusion.60), channel_id=1, source_target_pairs={{16,0},{17,1},{18,2},{19,3},{20,4},{21,5},{22,6},{23,7},{24,8},{25... | collective-permute-start | bytes 1572872 | tf_op jit(solution)/shard_map/ppermute | solution.py:13
  493.0 0.8 copy-start.8
  493.9 162.8 %reduce-scatter.7.cloned.1.call-start = ((), (), s32[]{:S(2)}) async-start(), calls=%async_computation.8 | async-start | bytes 4718592 | tf_op jit(solution)/shard_map/reduce_scatter | solution.py:69
  503.7 244.5 %reduce-scatter.11.cloned.1.call-start = ((), (), s32[]{:S(2)}) async-start(), calls=%async_computation.12 | async-start | bytes 4718592 | tf_op jit(solution)/shard_map/reduce_scatter | solution.py:69
  578.0 1.3 copy-start.12
  578.0 2.0 copy-start.14
  592.7 5.1 copy-start.13
  592.8 5.1 copy-start.15
  609.9 71.7 %collective-permute-start.2 = (bf16[1024,2048]{1,0:T(8,128)(2,1)}, bf16[1024,2048]{1,0:T(8,128)(2,1)}, u32[]{:S(2)}, u32[]{:S(2)}) collective-permute-start(bf16[1024,2048]{1,0:T(8,128)(2,1)} %get-tuple-element.119), channel_id=1, source_target_pairs={{0,1},{1,0},{2,3},{3,2},{4,5},{5,4},{6,7},{7,6},{8,9},{9,8},{10,11... | collective-permute-start | bytes 12582920 | tf_op jit(solution)/shard_map/ppermute | solution.py:221
  609.9 46.8 %copy-start.6 = (bf16[128,2048]{1,0:T(8,128)(2,1)S(1)}, bf16[128,2048]{1,0:T(8,128)(2,1)}, u32[]{:S(2)}) copy-start(bf16[128,2048]{1,0:T(8,128)(2,1)} %copy-done.5) | copy-start | bytes 1572868
  616.2 60.2 %collective-permute-start.3 = (bf16[512,2048]{1,0:T(8,128)(2,1)}, bf16[512,2048]{1,0:T(8,128)(2,1)}, u32[]{:S(2)}, u32[]{:S(2)}) collective-permute-start(bf16[512,2048]{1,0:T(8,128)(2,1)} %get-tuple-element.121), channel_id=1, source_target_pairs={{0,1},{1,0},{2,3},{3,2},{4,5},{5,4},{6,7},{7,6},{8,9},{9,8},{10,11... | collective-permute-start | bytes 6291464 | tf_op jit(solution)/shard_map/ppermute | solution.py:221
  676.4 6.2 copy-start.3
  686.8 61.5 %copy-start.2 = (bf16[8,16,2048]{2,1,0:T(8,128)(2,1)S(1)}, bf16[8,16,2048]{2,1,0:T(8,128)(2,1)}, u32[]{:S(2)}) copy-start(bf16[8,16,2048]{2,1,0:T(8,128)(2,1)} %param.16) | copy-start | bytes 1572868
  686.8 61.5 %copy-start.21 = (f32[128]{0:T(128)S(1)}, f32[128]{0:T(128)}, u32[]{:S(2)}) copy-start(f32[128]{0:T(128)} %copy-done.20) | copy-start | bytes 1540
  686.8 62.8 %copy-start.9 = (bf16[128,2048]{1,0:T(8,128)(2,1)S(1)}, bf16[128,2048]{1,0:T(8,128)(2,1)}, u32[]{:S(2)}) copy-start(bf16[128,2048]{1,0:T(8,128)(2,1)} %copy-done.8) | copy-start | bytes 1572868
  686.8 62.8 %copy-start.17 = (bf16[128,2048]{1,0:T(8,128)(2,1)S(1)}, bf16[128,2048]{1,0:T(8,128)(2,1)}, u32[]{:S(2)}) copy-start(bf16[128,2048]{1,0:T(8,128)(2,1)} %copy-done.16) | copy-start | bytes 1572868
Sparse Core Ops, SparseCore 0:
  10.7 75.4 all-gather.4
  109.3 86.8 reduce-scatter.4
  212.9 73.9 all-gather.6
  288.9 71.3 all-gather.8
  387.3 86.8 reduce-scatter.8
  494.0 72.0 all-gather.10
  569.8 86.8 reduce-scatter.6
  660.3 87.9 reduce-scatter.10
where the time goes:
time: 768 us; the launch traced here: 759 us
  waiting for transfers between devices  546 us (71%)
  matrix products  125 us (16%)
  other arithmetic  36.8 us (5%)
  local copies, waits for them, and re-layouts  22.3 us (3%)
  between operations  14.9 us (2%)
  starting transfers between devices  13.5 us (2%)
    reduce_scatter x4, waiting for transfers between devices, scatter(): return lax.psum_scatter(rows, 'expert', scatter_dimension=0, tiled=True)  272 us
    all_gather x4, waiting for transfers between devices, gather(): return lax.all_gather(rows, 'expert', axis=0, tiled=True)  249 us
    dot_general x4, matrix products, contract(): lax.dot_general(left, right, (((0,), (0,)), ((), ())), preferred_element_...  32.7 us
    dot_general x2, matrix products, on_device(): jnp.dot(gathered, w_in, preferred_element_type=jnp.float32)  27.3 us
    dot_general x2, matrix products, on_device(): lax.dot_general(pre_grad, w_in, (((1,), (1,)), ((), ())), preferred_eleme...  25.3 us
    ppermute x2, waiting for transfers between devices, from_behind(): return lax.ppermute(block, axis, route)  24.6 us
    dot_general x2, matrix products, on_device(): lax.dot_general(gathered, w_out, (((1,), (1,)), ((), ())), preferred_elem...  24.2 us
    dot_general x2, matrix products, on_device(): jnp.dot(act, w_out, preferred_element_type=jnp.float32).astype(jnp.bfloat16)  15.5 us
  transfers between devices with their start and end apart: 13, of which 11 were waited for; matrix products, arithmetic and copies ran while one was open for 15% of the time, Pallas kernels for 0%

commit v1 on v0

--- a/solution.py
+++ b/solution.py
@@ -5,6 +5,19 @@
 
 epsilon = 1e-06
 ROW_LIMIT = 1024
+
+
+def collect(value, axis, dim):
+    ways = lax.axis_size(axis)
+    up = [(d, (d + 1) % ways) for d in range(ways)]
+    down = [(d, (d - 1) % ways) for d in range(ways)]
+    earlier, later = ([value], [value])
+    for _ in range(ways // 2):
+        earlier.append(lax.ppermute(earlier[-1], axis, up))
+    for _ in range((ways - 1) // 2):
+        later.append(lax.ppermute(later[-1], axis, down))
+    line = jnp.concatenate([*earlier[::-1], *later[1:]], axis=dim)
+    return jnp.roll(line, (lax.axis_index(axis) - ways // 2) * value.shape[dim], axis=dim)
 
 
 def from_behind(block, axis, distance):
@@ -63,7 +76,7 @@
         return jnp.repeat(rows, hidden_units, axis=1)
 
     def gather(rows):
-        return lax.all_gather(rows, "expert", axis=0, tiled=True)
+        return collect(rows, "expert", 0)
 
     def scatter(rows):
         return lax.psum_scatter(rows, "expert", scatter_dimension=0, tiled=True)

time: 768 us -> 797 us (1.038)
  starting transfers between devices: 13.5 us -> 93 us
  waiting for transfers between devices: 546 us -> 481 us
  other arithmetic: 36.8 us -> 53.2 us
    all_gather x4 -> x0, waiting for transfers between devices: 249 us -> none  [gather(): return lax.all_gather(rows, 'expert', axis=0, tiled=True)]
    ppermute x0 -> x28, waiting for transfers between devices: none -> 235 us  [the longest x16 210 us: collect(): earlier.append(lax.ppermute(earlier[-1], axis, up))]
    ppermute x0 -> x28, starting transfers between devices: none -> 82.7 us  [the longest x12 54.1 us: collect(): later.append(lax.ppermute(later[-1], axis, down))]
    reduce_scatter x4, waiting for transfers between devices: 272 us -> 221 us  [scatter(): return lax.psum_scatter(rows, 'expert', scatter_dimension=0, tiled=True)]
    concatenate x0 -> x3, other arithmetic: none -> 18.6 us  [collect(): jnp.roll(line, (lax.axis_index(axis) - ways // 2) * value.shape[dim], axi...]
    unnamed x49 -> x100, local copies, waits for them, and re-layouts: 12.6 us -> 17.8 us
  transfers between devices with their start and end apart: 13 -> 37, of which waited for: 11 -> 24; matrix products, arithmetic and copies ran while one was open for 15% -> 14% of each run, Pallas kernels for 0% -> 0%
where the time goes in v1:
time: 797 us; the launch traced here: 792 us
  waiting for transfers between devices  481 us (60%)
  matrix products  123 us (15%)
  starting transfers between devices  93 us (12%)
  other arithmetic  53.2 us (7%)
  local copies, waits for them, and re-layouts  27 us (3%)
  between operations  14.8 us (2%)
    reduce_scatter x4, waiting for transfers between devices, scatter(): return lax.psum_scatter(rows, 'expert', scatter_dimension=0, tiled=True)  221 us
    ppermute x16, waiting for transfers between devices, collect(): earlier.append(lax.ppermute(earlier[-1], axis, up))  210 us
    ppermute x12, starting transfers between devices, collect(): later.append(lax.ppermute(later[-1], axis, down))  54.1 us
    dot_general x4, matrix products, contract(): lax.dot_general(left, right, (((0,), (0,)), ((), ())), preferred_element_...  32.8 us
    ppermute x16, starting transfers between devices, collect(): earlier.append(lax.ppermute(earlier[-1], axis, up))  28.6 us
    dot_general x2, matrix products, on_device(): jnp.dot(gathered, w_in, preferred_element_type=jnp.float32)  27.6 us
    dot_general x2, matrix products, on_device(): lax.dot_general(pre_grad, w_in, (((1,), (1,)), ((), ())), preferred_eleme...  27 us
    ppermute x2, waiting for transfers between devices, from_behind(): return lax.ppermute(block, axis, route)  24.6 us
  transfers between devices with their start and end apart: 37, of which 24 were waited for; matrix products, arithmetic and copies ran while one was open for 14% of the time, Pallas kernels for 0%

profile of v1, /device:TPU:0, one launch (start us, length us, event | category | flops | bytes accessed | tf_op | source)
XLA Modules:
  0.0 792.5 jit_solution(1853880099463762897)
XLA Ops:
  7.2 3.0 collective-permute-start.15
  14.4 11.9 %collective-permute-done.15 = bf16[128,2048]{1,0:T(8,128)(2,1)S(1)} collective-permute-done((bf16[128,2048]{1,0:T(8,128)(2,1)}, bf16[128,2048]{1,0:T(8,128)(2,1)S(1)}, u32[]{:S(2)}, u32[]{:S(2)}) %collective-permute-start.15) | collective-permute-done | bytes 524320 | tf_op jit(solution)/shard_map/ppermute | solution.py:16
  26.2 4.7 collective-permute-start.19
  31.0 25.5 %collective-permute-done = bf16[128,2048]{1,0:T(8,128)(2,1)S(1)} collective-permute-done((bf16[128,2048]{1,0:T(8,128)(2,1)S(1)}, bf16[128,2048]{1,0:T(8,128)(2,1)S(1)}, u32[]{:S(2)}, u32[]{:S(2)}) %collective-permute-start) | collective-permute-done | bytes 524320 | tf_op jit(solution)/shard_map/ppermute | solution.py:16
  56.4 2.5 collective-permute-start.1
  58.9 8.8 %collective-permute-done.16 = bf16[128,2048]{1,0:T(8,128)(2,1)S(1)} collective-permute-done((bf16[128,2048]{1,0:T(8,128)(2,1)S(1)}, bf16[128,2048]{1,0:T(8,128)(2,1)S(1)}, u32[]{:S(2)}, u32[]{:S(2)}) %collective-permute-start.16) | collective-permute-done | bytes 524320 | tf_op jit(solution)/shard_map/ppermute | solution.py:16
  67.7 2.5 collective-permute-start.17
  71.8 4.9 all-to-all-start
  76.7 4.7 collective-permute-start.20
  81.4 11.5 %collective-permute-done.4 = bf16[128,2048]{1,0:T(8,128)(2,1)S(1)} collective-permute-done((bf16[128,2048]{1,0:T(8,128)(2,1)S(1)}, bf16[128,2048]{1,0:T(8,128)(2,1)S(1)}, u32[]{:S(2)}, u32[]{:S(2)}) %collective-permute-start.4) | collective-permute-done | bytes 524320 | tf_op jit(solution)/shard_map/ppermute | solution.py:18
  95.0 17.7 %collective-permute-done.17 = bf16[128,2048]{1,0:T(8,128)(2,1)} collective-permute-done((bf16[128,2048]{1,0:T(8,128)(2,1)S(1)}, bf16[128,2048]{1,0:T(8,128)(2,1)}, u32[]{:S(2)}, u32[]{:S(2)}) %collective-permute-start.17) | collective-permute-done | bytes 524320 | tf_op jit(solution)/shard_map/ppermute | solution.py:16
  112.7 2.6 collective-permute-start.18
  115.2 6.0 slice_bitcast_fusion.1
  125.4 3.1 collective-permute-start.21
  128.5 9.5 %collective-permute-done.5 = bf16[128,2048]{1,0:T(8,128)(2,1)} collective-permute-done((bf16[128,2048]{1,0:T(8,128)(2,1)S(1)}, bf16[128,2048]{1,0:T(8,128)(2,1)}, u32[]{:S(2)}, u32[]{:S(2)}) %collective-permute-start.5) | collective-permute-done | bytes 524320 | tf_op jit(solution)/shard_map/ppermute | solution.py:18
  140.3 17.4 %collective-permute-done.18 = bf16[128,2048]{1,0:T(8,128)(2,1)} collective-permute-done((bf16[128,2048]{1,0:T(8,128)(2,1)}, bf16[128,2048]{1,0:T(8,128)(2,1)}, u32[]{:S(2)}, u32[]{:S(2)}) %collective-permute-start.18) | collective-permute-done | bytes 524320 | tf_op jit(solution)/shard_map/ppermute | solution.py:16
  160.1 7.8 collective-permute-done.3
  172.5 8.3 %fusion.53 = (bf16[1024,2048]{1,0:T(8,128)(2,1)}, bf16[1024,2048]{1,0:T(8,128)(2,1)S(1)}) fusion(s32[]{:T(128)S(6)} %select_n.82, bf16[1024,2048]{1,0:T(8,128)(2,1)S(1)} %constant_dynamic-update-slice_fusion.16, bf16[1024,2048]{1,0:T(8,128)(2,1)S(1)} %constant_dynamic-update-slice_fusion), kind=kLoop, calls=%fused_computation.87 | loop fusion | flops 16777216 | bytes 16777220 | tf_op jit(solution)/shard_map/jit(_roll_dynamic)/concatenate | solution.py:20
  180.8 13.1 %convolution_convert_fusion.5 = bf16[1024,2048]{1,0:T(8,128)(2,1)S(1)} fusion(bf16[1024,2048]{1,0:T(8,128)(2,1)S(1)} %get-tuple-element.118, bf16[2048,512]{1,0:T(8,128)(2,1)} %get-tuple-element.116, bf16[2048,512]{1,0:T(8,128)(2,1)} %get-tuple-element.115, bf16[2048,512]{1,0:T(8,128)(2,1)} %get-tuple-element.119, bf16[2048,512]{1,0:T(8,128)(2,1)} %get-tuple-element.120), kind=kOutput, calls=%fused_computation.96 | convolution fusion | flops 8625586176 | bytes 16777216 | tf_op jit(solution)/shard_map/dot_general | solution.py:115
  198.5 6.1 convolution_convert_fusion.7
  204.7 90.5 %reduce-scatter.5.cloned.1.call-done = bf16[128,2048]{1,0:T(8,128)(2,1)} async-done(((bf16[1024,2048]{1,0:T(8,128)(2,1)}), bf16[128,2048]{1,0:T(8,128)(2,1)}) %reduce-scatter.5.cloned.1.call-update) | async-done | bytes 524304 | tf_op jit(solution)/shard_map/reduce_scatter | solution.py:82
  296.4 3.4 collective-permute-start.7
  299.8 10.8 %collective-permute-done.7 = bf16[128,2048]{1,0:T(8,128)(2,1)S(1)} collective-permute-done((bf16[128,2048]{1,0:T(8,128)(2,1)S(1)}, bf16[128,2048]{1,0:T(8,128)(2,1)S(1)}, u32[]{:S(2)}, u32[]{:S(2)}) %collective-permute-start.7) | collective-permute-done | bytes 524320 | tf_op jit(solution)/shard_map/ppermute | solution.py:26
  312.5 13.7 %collective-permute-done.8 = bf16[128,2048]{1,0:T(8,128)(2,1)S(1)} collective-permute-done((bf16[128,2048]{1,0:T(8,128)(2,1)S(1)}, bf16[128,2048]{1,0:T(8,128)(2,1)S(1)}, u32[]{:S(2)}, u32[]{:S(2)}) %collective-permute-start.8) | collective-permute-done | bytes 524320 | tf_op jit(solution)/shard_map/ppermute | solution.py:16
  326.1 4.7 collective-permute-start.12
  330.9 15.9 %collective-permute-done.9 = bf16[128,2048]{1,0:T(8,128)(2,1)S(1)} collective-permute-done((bf16[128,2048]{1,0:T(8,128)(2,1)S(1)}, bf16[128,2048]{1,0:T(8,128)(2,1)S(1)}, u32[]{:S(2)}, u32[]{:S(2)}) %collective-permute-start.9) | collective-permute-done | bytes 524320 | tf_op jit(solution)/shard_map/ppermute | solution.py:16
  346.7 3.0 collective-permute-start.10
  349.8 12.4 %collective-permute-start.13 = (bf16[128,2048]{1,0:T(8,128)(2,1)S(1)}, bf16[128,2048]{1,0:T(8,128)(2,1)S(1)}, u32[]{:S(2)}, u32[]{:S(2)}) collective-permute-start(bf16[128,2048]{1,0:T(8,128)(2,1)S(1)} %collective-permute-done.12), channel_id=1, source_target_pairs={{0,14},{2,0},{4,2},{6,4},{8,6},{10,8},{12,10},{14,12},{1,15},{3,1}... | collective-permute-start | bytes 1572872 | tf_op jit(solution)/shard_map/ppermute | solution.py:18
  362.1 8.6 %collective-permute-done.10 = bf16[128,2048]{1,0:T(8,128)(2,1)S(1)} collective-permute-done((bf16[128,2048]{1,0:T(8,128)(2,1)S(1)}, bf16[128,2048]{1,0:T(8,128)(2,1)S(1)}, u32[]{:S(2)}, u32[]{:S(2)}) %collective-permute-start.10) | collective-permute-done | bytes 524320 | tf_op jit(solution)/shard_map/ppermute | solution.py:16
  370.7 2.5 collective-permute-start.11
  373.5 13.7 %collective-permute-start.14 = (bf16[128,2048]{1,0:T(8,128)(2,1)S(1)}, bf16[128,2048]{1,0:T(8,128)(2,1)S(1)}, u32[]{:S(2)}, u32[]{:S(2)}) collective-permute-start(bf16[128,2048]{1,0:T(8,128)(2,1)S(1)} %collective-permute-done.13), channel_id=1, source_target_pairs={{0,14},{2,0},{4,2},{6,4},{8,6},{10,8},{12,10},{14,12},{1,15},{3,1}... | collective-permute-start | bytes 1572872 | tf_op jit(solution)/shard_map/ppermute | solution.py:18
  387.2 7.3 collective-permute-done.11
  395.0 2.8 collective-permute-done.14
  397.8 5.7 fusion.54
  403.5 14.4 %convolution_convert_fusion.4 = bf16[1024,2048]{1,0:T(8,128)(2,1)} fusion(bf16[1024,2048]{1,0:T(8,128)(2,1)} %fusion.54, bf16[2048,512]{1,0:T(8,128)(2,1)} %get-tuple-element.116, bf16[2048,512]{1,0:T(8,128)(2,1)S(1)} %copy-done.27, bf16[2048,512]{1,0:T(8,128)(2,1)} %get-tuple-element.119, bf16[2048,512]{1,0:T(8,128)(2,1)} %get-tuple-element.120), kind=kOutput, calls=%fused_computation.95 | convolution fusion | flops 8625586176 | bytes 16777216 | tf_op jit(solution)/shard_map/dot_general | solution.py:115
  417.9 10.9 %fusion.39 = (bf16[1024,1024]{1,0:T(8,128)(2,1)}, bf16[1024,1024]{1,0:T(8,128)(2,1)}, bf16[1024,1024]{1,0:T(8,128)(2,1)S(1)}) fusion(bf16[1024,2048]{1,0:T(8,128)(2,1)} %convolution_convert_fusion.4, f32[1024,1024]{1,0:T(8,128)S(1)} %bitcast.78, bf16[1024,2048]{1,0:T(8,128)(2,1)S(1)} %copy-done.8, bf16[1024,2048]{1,0:T(8,128)(2,1)} %bitcast.99), kind=kOutput, calls=%fused_computation.73 | convolution fusion | flops 4315938816 | bytes 23068672 | tf_op jit(solution)/shard_map/dot_general | solution.py:147
  428.9 14.7 %convolution_convert_fusion.3 = bf16[1024,2048]{1,0:T(8,128)(2,1)} fusion(bf16[1024,1024]{1,0:T(8,128)(2,1)} %get-tuple-element.107, bf16[1024,1024]{1,0:T(8,128)(2,1)} %get-tuple-element.106, bf16[2048,512]{1,0:T(8,128)(2,1)} %get-tuple-element.116, bf16[2048,512]{1,0:T(8,128)(2,1)} %get-tuple-element.115, bf16[2048,512]{1,0:T(8,128)(2,1)} %get-tuple-element.119, ...), kind=kOutput, calls=%fused_computation.94 | convolution fusion | flops 8633974784 | bytes 16777216 | tf_op jit(solution)/shard_map/dot_general | solution.py:159
  443.7 91.3 %reduce-scatter.9.cloned.1.call-done = bf16[128,2048]{1,0:T(8,128)(2,1)} async-done(((bf16[1024,2048]{1,0:T(8,128)(2,1)}), bf16[128,2048]{1,0:T(8,128)(2,1)}) %reduce-scatter.9.cloned.1.call-update) | async-done | bytes 524304 | tf_op jit(solution)/shard_map/reduce_scatter | solution.py:82
  539.1 13.9 %collective-permute-done.22 = bf16[128,2048]{1,0:T(8,128)(2,1)S(1)} collective-permute-done((bf16[128,2048]{1,0:T(8,128)(2,1)S(1)}, bf16[128,2048]{1,0:T(8,128)(2,1)S(1)}, u32[]{:S(2)}, u32[]{:S(2)}) %collective-permute-start.22) | collective-permute-done | bytes 524320 | tf_op jit(solution)/shard_map/ppermute | solution.py:26
  554.5 8.3 %convolution_convert_fusion.6 = bf16[1024,2048]{1,0:T(8,128)(2,1)} fusion(bf16[1024,1024]{1,0:T(8,128)(2,1)S(1)} %get-tuple-element.112, bf16[1024,2048]{1,0:T(8,128)(2,1)} %bitcast.100), kind=kOutput, calls=%fused_computation.97 | convolution fusion | flops 4297064448 | bytes 10485760 | tf_op jit(solution)/shard_map/dot_general | solution.py:118
  562.8 5.4 collective-permute-done.23
  568.2 4.7 collective-permute-start.27
  572.9 21.8 %collective-permute-done.24 = bf16[128,2048]{1,0:T(8,128)(2,1)S(1)} collective-permute-done((bf16[128,2048]{1,0:T(8,128)(2,1)}, bf16[128,2048]{1,0:T(8,128)(2,1)S(1)}, u32[]{:S(2)}, u32[]{:S(2)}) %collective-permute-start.24) | collective-permute-done | bytes 524320 | tf_op jit(solution)/shard_map/ppermute | solution.py:16
  594.7 2.4 collective-permute-start.25
  599.5 24.4 %collective-permute-done.25 = bf16[128,2048]{1,0:T(8,128)(2,1)S(1)} collective-permute-done((bf16[128,2048]{1,0:T(8,128)(2,1)S(1)}, bf16[128,2048]{1,0:T(8,128)(2,1)S(1)}, u32[]{:S(2)}, u32[]{:S(2)}) %collective-permute-start.25) | collective-permute-done | bytes 524320 | tf_op jit(solution)/shard_map/ppermute | solution.py:16
  623.8 2.5 collective-permute-start.26
  626.3 2.4 collective-permute-start.29
  628.8 24.6 %collective-permute-done.26 = bf16[128,2048]{1,0:T(8,128)(2,1)S(1)} collective-permute-done((bf16[128,2048]{1,0:T(8,128)(2,1)S(1)}, bf16[128,2048]{1,0:T(8,128)(2,1)S(1)}, u32[]{:S(2)}, u32[]{:S(2)}) %collective-permute-start.26) | collective-permute-done | bytes 524320 | tf_op jit(solution)/shard_map/ppermute | solution.py:16
  655.0 4.6 fusion.52
  659.7 10.1 %fusion.34 = (bf16[1024,1024]{1,0:T(8,128)(2,1)S(1)}, bf16[1024,1024]{1,0:T(8,128)(2,1)S(1)}) fusion(bf16[1024,2048]{1,0:T(8,128)(2,1)S(1)} %copy-done.12, f32[1024,1024]{1,0:T(8,128)S(1)} %bitcast.79, bf16[1024,2048]{1,0:T(8,128)(2,1)S(1)} %fusion.52, bf16[1024,2048]{1,0:T(8,128)(2,1)} %bitcast.101), kind=kOutput, calls=%fused_computation.68 | convolution fusion | flops 4311744512 | bytes 20971520 | tf_op jit(solution)/shard_map/dot_general | solution.py:147
  671.9 12.3 %convolution_convert_fusion.2 = bf16[1024,2048]{1,0:T(8,128)(2,1)} fusion(bf16[1024,1024]{1,0:T(8,128)(2,1)S(1)} %get-tuple-element.105, bf16[1024,1024]{1,0:T(8,128)(2,1)S(1)} %get-tuple-element.104, bf16[2048,512]{1,0:T(8,128)(2,1)} %get-tuple-element.116, bf16[2048,512]{1,0:T(8,128)(2,1)S(1)} %copy-done.28, bf16[2048,512]{1,0:T(8,128)(2,1)} %get-tuple-element.119, ...), kind=kOutput, calls=%fused_computation.93 | convolution fusion | flops 8633974784 | bytes 16777216 | tf_op jit(solution)/shard_map/dot_general | solution.py:159
  685.8 4.3 pad_maximum_fusion.1
  690.1 2.4 pad_maximum_fusion.2
  692.5 10.0 %conditional.13 = (bf16[1024,2048]{1,0:T(8,128)(2,1)}) conditional(s32[]{:T(128)} %clamp.2, (s32[]{:T(128)}, bf16[1024,2048]{1,0:T(8,128)(2,1)}, bf16[1024,2048]{1,0:T(8,128)(2,1)}) %tuple.85, (s32[]{:T(128)}, bf16[1024,2048]{1,0:T(8,128)(2,1)}, bf16[1024,2048]{1,0:T(8,128)(2,1)}) %tuple.46), branch_computations={%region_11.13_spmd, %region_12.14_spmd} | conditional | flops 4294967296 | bytes 10485818
  692.5 9.6 %fusion.4 = bf16[1024,2048]{1,0:T(8,128)(2,1)} fusion(bf16[1024,2048]{1,0:T(8,128)(2,1)} %get-tuple-element.75, bf16[1024,2048]{1,0:T(8,128)(2,1)} %get-tuple-element.73, s32[]{:T(128)S(6)} %select_n.55), kind=kOutput, calls=%fused_computation.6 | convolution fusion | flops 4294967296 | bytes 10485764 | tf_op jit(solution)/shard_map/cond/branch_0_fun/dot_general | solution.py:178
  702.6 6.1 conditional.15
  702.8 5.9 fusion.20
  711.2 11.0 %conditional.12 = (f32[1024,2048]{1,0:T(8,128)}) conditional(s32[]{:T(128)} %clamp.2, (s32[]{:T(128)}, bf16[1024,2048]{1,0:T(8,128)(2,1)}, bf16[1024,2048]{1,0:T(8,128)(2,1)}) %tuple.86, (s32[]{:T(128)}, bf16[1024,2048]{1,0:T(8,128)(2,1)}, bf16[1024,2048]{1,0:T(8,128)(2,1)}) %tuple.44), branch_computations={%region_9.11_spmd, %region_10.12_spmd} | conditional | flops 4299161600 | bytes 14680122 | solution.py:210
  711.4 10.8 %convert_convert_fusion = f32[1024,2048]{1,0:T(8,128)} fusion(bf16[1024,2048]{1,0:T(8,128)(2,1)} %get-tuple-element.69, bf16[1024,2048]{1,0:T(8,128)(2,1)} %get-tuple-element.67, s32[]{:T(128)S(6)} %select_n.53), kind=kOutput, calls=%fused_computation | convolution fusion | flops 4299161600 | bytes 14680068 | tf_op jit(solution)/shard_map/cond/branch_0_fun/dot_general | solution.py:178
  722.2 6.9 conditional.14
  722.4 6.5 fusion.10
  729.1 5.1 add_convert_fusion.1
  735.3 3.7 add_convert_fusion
  742.5 39.5 %reduce-scatter.11.cloned.1.call-done = bf16[128,2048]{1,0:T(8,128)(2,1)} async-done(((bf16[1024,2048]{1,0:T(8,128)(2,1)}), bf16[128,2048]{1,0:T(8,128)(2,1)}) %reduce-scatter.11.cloned.1.call-update) | async-done | bytes 524304 | tf_op jit(solution)/shard_map/reduce_scatter | solution.py:82
  (169 shorter events, 54.0 us)
Async XLA Ops:
  7.2 19.0 %collective-permute-start.15 = (bf16[128,2048]{1,0:T(8,128)(2,1)}, bf16[128,2048]{1,0:T(8,128)(2,1)S(1)}, u32[]{:S(2)}, u32[]{:S(2)}) collective-permute-start(bf16[128,2048]{1,0:T(8,128)(2,1)} %bitcast.82), channel_id=1, source_target_pairs={{0,2},{2,4},{4,6},{6,8},{8,10},{10,12},{12,14},{14,0},{1,3},{3,5},... | collective-permute-start | bytes 1572872 | tf_op jit(solution)/shard_map/ppermute | solution.py:16
  12.7 43.7 %collective-permute-start = (bf16[128,2048]{1,0:T(8,128)(2,1)S(1)}, bf16[128,2048]{1,0:T(8,128)(2,1)S(1)}, u32[]{:S(2)}, u32[]{:S(2)}) collective-permute-start(bf16[128,2048]{1,0:T(8,128)(2,1)S(1)} %fusion.70), channel_id=1, source_target_pairs={{0,2},{2,4},{4,6},{6,8},{8,10},{10,12},{12,14},{14,0},{1,3},{3,5},... | collective-permute-start | bytes 1572872 | tf_op jit(solution)/shard_map/ppermute | solution.py:16
  26.2 41.4 %collective-permute-start.16 = (bf16[128,2048]{1,0:T(8,128)(2,1)S(1)}, bf16[128,2048]{1,0:T(8,128)(2,1)S(1)}, u32[]{:S(2)}, u32[]{:S(2)}) collective-permute-start(bf16[128,2048]{1,0:T(8,128)(2,1)S(1)} %collective-permute-done.15), channel_id=1, source_target_pairs={{0,2},{2,4},{4,6},{6,8},{8,10},{10,12},{12,14},{14,0},{1,3},{3,5},... | collective-permute-start | bytes 1572872 | tf_op jit(solution)/shard_map/ppermute | solution.py:16
  26.2 50.5 %collective-permute-start.19 = (bf16[128,2048]{1,0:T(8,128)(2,1)}, bf16[128,2048]{1,0:T(8,128)(2,1)S(1)}, u32[]{:S(2)}, u32[]{:S(2)}) collective-permute-start(bf16[128,2048]{1,0:T(8,128)(2,1)} %bitcast.83), channel_id=1, source_target_pairs={{0,14},{2,0},{4,2},{6,4},{8,6},{10,8},{12,10},{14,12},{1,15},{3,1}... | collective-permute-start | bytes 1572872 | tf_op jit(solution)/shard_map/ppermute | solution.py:18
  30.9 62.0 %collective-permute-start.4 = (bf16[128,2048]{1,0:T(8,128)(2,1)S(1)}, bf16[128,2048]{1,0:T(8,128)(2,1)S(1)}, u32[]{:S(2)}, u32[]{:S(2)}) collective-permute-start(bf16[128,2048]{1,0:T(8,128)(2,1)S(1)} %fusion.70), channel_id=1, source_target_pairs={{0,14},{2,0},{4,2},{6,4},{8,6},{10,8},{12,10},{14,12},{1,15},{3,1}... | collective-permute-start | bytes 1572872 | tf_op jit(solution)/shard_map/ppermute | solution.py:18
  56.4 37.2 %collective-permute-start.1 = (bf16[128,2048]{1,0:T(8,128)(2,1)S(1)}, bf16[128,2048]{1,0:T(8,128)(2,1)}, u32[]{:S(2)}, u32[]{:S(2)}) collective-permute-start(bf16[128,2048]{1,0:T(8,128)(2,1)S(1)} %collective-permute-done), channel_id=1, source_target_pairs={{0,2},{2,4},{4,6},{6,8},{8,10},{10,12},{12,14},{14,0},{1,3},{3,5},... | collective-permute-start | bytes 1572872 | tf_op jit(solution)/shard_map/ppermute | solution.py:16
  67.6 53.6 %copy-start.29 = (bf16[128,2048]{1,0:T(8,128)(2,1)}, bf16[128,2048]{1,0:T(8,128)(2,1)S(1)}, u32[]{:S(2)}) copy-start(bf16[128,2048]{1,0:T(8,128)(2,1)S(1)} %collective-permute-done.16) | copy-start | bytes 1572868
  67.7 45.0 %collective-permute-start.17 = (bf16[128,2048]{1,0:T(8,128)(2,1)S(1)}, bf16[128,2048]{1,0:T(8,128)(2,1)}, u32[]{:S(2)}, u32[]{:S(2)}) collective-permute-start(bf16[128,2048]{1,0:T(8,128)(2,1)S(1)} %collective-permute-done.16), channel_id=1, source_target_pairs={{0,2},{2,4},{4,6},{6,8},{8,10},{10,12},{12,14},{14,0},{1,3},{3,5},... | collective-permute-start | bytes 1572872 | tf_op jit(solution)/shard_map/ppermute | solution.py:16
  71.8 49.5 %all-to-all-start = ((f32[8,1,256]{2,1,0:T(1,128)}), f32[8,1,256]{2,1,0:T(1,128)S(1)}, u32[]{:S(2)}, u32[]{:S(2)}) async-start(f32[8,1,256]{2,1,0:T(1,128)} %reshape.77), calls=%async_computation | async-start | bytes 16384 | tf_op jit(solution)/shard_map/all_to_all | solution.py:42
  76.7 218.5 %reduce-scatter.5.cloned.1.call-start = ((), (), s32[]{:S(2)}) async-start(), calls=%async_computation.5 | async-start | bytes 4718592 | tf_op jit(solution)/shard_map/reduce_scatter | solution.py:82
  76.7 48.7 %collective-permute-start.20 = (bf16[128,2048]{1,0:T(8,128)(2,1)S(1)}, bf16[128,2048]{1,0:T(8,128)(2,1)}, u32[]{:S(2)}, u32[]{:S(2)}) collective-permute-start(bf16[128,2048]{1,0:T(8,128)(2,1)S(1)} %collective-permute-done.19), channel_id=1, source_target_pairs={{0,14},{2,0},{4,2},{6,4},{8,6},{10,8},{12,10},{14,12},{1,15},{3,1}... | collective-permute-start | bytes 1572872 | tf_op jit(solution)/shard_map/ppermute | solution.py:18
  92.9 45.1 %collective-permute-start.5 = (bf16[128,2048]{1,0:T(8,128)(2,1)S(1)}, bf16[128,2048]{1,0:T(8,128)(2,1)}, u32[]{:S(2)}, u32[]{:S(2)}) collective-permute-start(bf16[128,2048]{1,0:T(8,128)(2,1)S(1)} %collective-permute-done.4), channel_id=1, source_target_pairs={{0,14},{2,0},{4,2},{6,4},{8,6},{10,8},{12,10},{14,12},{1,15},{3,1}... | collective-permute-start | bytes 1572872 | tf_op jit(solution)/shard_map/ppermute | solution.py:18
  93.6 45.0 %collective-permute-start.2 = (bf16[128,2048]{1,0:T(8,128)(2,1)}, bf16[128,2048]{1,0:T(8,128)(2,1)}, u32[]{:S(2)}, u32[]{:S(2)}) collective-permute-start(bf16[128,2048]{1,0:T(8,128)(2,1)} %collective-permute-done.1), channel_id=1, source_target_pairs={{0,2},{2,4},{4,6},{6,8},{8,10},{10,12},{12,14},{14,0},{1,3},{3,5},... | collective-permute-start | bytes 1572872 | tf_op jit(solution)/shard_map/ppermute | solution.py:16
  112.7 45.1 %collective-permute-start.18 = (bf16[128,2048]{1,0:T(8,128)(2,1)}, bf16[128,2048]{1,0:T(8,128)(2,1)}, u32[]{:S(2)}, u32[]{:S(2)}) collective-permute-start(bf16[128,2048]{1,0:T(8,128)(2,1)} %collective-permute-done.17), channel_id=1, source_target_pairs={{0,2},{2,4},{4,6},{6,8},{8,10},{10,12},{12,14},{14,0},{1,3},{3,5},... | collective-permute-start | bytes 1572872 | tf_op jit(solution)/shard_map/ppermute | solution.py:16
  124.4 35.5 %copy-start.30 = (bf16[128,2048]{1,0:T(8,128)(2,1)S(1)}, bf16[128,2048]{1,0:T(8,128)(2,1)}, u32[]{:S(2)}) copy-start(bf16[128,2048]{1,0:T(8,128)(2,1)} %copy-done.29) | copy-start | bytes 1572868
  125.4 68.6 %copy-start = (f32[128,8,2,512]{3,1,2,0:T(8,128)}, f32[128,8,2,512]{3,1,2,0:T(8,128)S(1)}, u32[]{:S(2)}) copy-start(f32[128,8,2,512]{3,1,2,0:T(8,128)S(1)} %copy.35) | copy-start | bytes 12582916
  125.4 34.6 %copy-start.16 = (bf16[8,16,2048]{2,1,0:T(8,128)(2,1)S(1)}, bf16[8,16,2048]{2,1,0:T(8,128)(2,1)}, u32[]{:S(2)}) copy-start(bf16[8,16,2048]{2,1,0:T(8,128)(2,1)} %param.19) | copy-start | bytes 1572868
  125.4 47.0 %collective-permute-start.21 = (bf16[128,2048]{1,0:T(8,128)(2,1)}, bf16[128,2048]{1,0:T(8,128)(2,1)S(1)}, u32[]{:S(2)}, u32[]{:S(2)}) collective-permute-start(bf16[128,2048]{1,0:T(8,128)(2,1)} %collective-permute-done.20), channel_id=1, source_target_pairs={{0,14},{2,0},{4,2},{6,4},{8,6},{10,8},{12,10},{14,12},{1,15},{3,1}... | collective-permute-start | bytes 1572872 | tf_op jit(solution)/shard_map/ppermute | solution.py:18
  138.0 34.5 %collective-permute-start.6 = (bf16[128,2048]{1,0:T(8,128)(2,1)}, bf16[128,2048]{1,0:T(8,128)(2,1)S(1)}, u32[]{:S(2)}, u32[]{:S(2)}) collective-permute-start(bf16[128,2048]{1,0:T(8,128)(2,1)} %collective-permute-done.5), channel_id=1, source_target_pairs={{0,14},{2,0},{4,2},{6,4},{8,6},{10,8},{12,10},{14,12},{1,15},{3,1}... | collective-permute-start | bytes 1572872 | tf_op jit(solution)/shard_map/ppermute | solution.py:18
  138.6 29.2 %collective-permute-start.3 = (bf16[128,2048]{1,0:T(8,128)(2,1)}, bf16[128,2048]{1,0:T(8,128)(2,1)S(1)}, u32[]{:S(2)}, u32[]{:S(2)}) collective-permute-start(bf16[128,2048]{1,0:T(8,128)(2,1)} %collective-permute-done.2), channel_id=1, source_target_pairs={{0,2},{2,4},{4,6},{6,8},{8,10},{10,12},{12,14},{14,0},{1,3},{3,5},... | collective-permute-start | bytes 1572872 | tf_op jit(solution)/shard_map/ppermute | solution.py:16
  180.8 13.1 %copy-start.9 = (bf16[1024,2048]{1,0:T(8,128)(2,1)}, bf16[1024,2048]{1,0:T(8,128)(2,1)S(1)}, u32[]{:S(2)}) copy-start(bf16[1024,2048]{1,0:T(8,128)(2,1)S(1)} %get-tuple-element.118) | copy-start | bytes 12582916
  194.0 4.5 copy-start.34
  204.6 90.6 %copy-start.3 = (bf16[8,16,2048]{2,1,0:T(8,128)(2,1)S(1)}, bf16[8,16,2048]{2,1,0:T(8,128)(2,1)}, u32[]{:S(2)}) copy-start(bf16[8,16,2048]{2,1,0:T(8,128)(2,1)} %param.18) | copy-start | bytes 1572868
  204.6 106.2 %copy-start.31 = (f32[1,2048]{1,0:T(1,128)S(1)}, f32[1,2048]{1,0:T(1,128)}, u32[]{:S(2)}) copy-start(f32[1,2048]{1,0:T(1,128)} %param.22) | copy-start | bytes 24580
  204.6 330.3 %reduce-scatter.9.cloned.1.call-start = ((), (), s32[]{:S(2)}) async-start(), calls=%async_computation.7 | async-start | bytes 4718592 | tf_op jit(solution)/shard_map/reduce_scatter | solution.py:82
  296.4 98.6 %copy-start.13 = (bf16[128,2048]{1,0:T(8,128)(2,1)}, bf16[128,2048]{1,0:T(8,128)(2,1)S(1)}, u32[]{:S(2)}) copy-start(bf16[128,2048]{1,0:T(8,128)(2,1)S(1)} %fusion.77) | copy-start | bytes 1572868
  296.4 14.2 %collective-permute-start.7 = (bf16[128,2048]{1,0:T(8,128)(2,1)S(1)}, bf16[128,2048]{1,0:T(8,128)(2,1)S(1)}, u32[]{:S(2)}, u32[]{:S(2)}) collective-permute-start(bf16[128,2048]{1,0:T(8,128)(2,1)S(1)} %fusion.77), channel_id=1, source_target_pairs={{0,16},{1,17},{2,18},{3,19},{4,20},{5,21},{6,22},{7,23},{8,24},{9,... | collective-permute-start | bytes 1572872 | tf_op jit(solution)/shard_map/ppermute | solution.py:26
  310.9 15.2 %collective-permute-start.8 = (bf16[128,2048]{1,0:T(8,128)(2,1)S(1)}, bf16[128,2048]{1,0:T(8,128)(2,1)S(1)}, u32[]{:S(2)}, u32[]{:S(2)}) collective-permute-start(bf16[128,2048]{1,0:T(8,128)(2,1)S(1)} %fusion.59), channel_id=1, source_target_pairs={{0,2},{2,4},{4,6},{6,8},{8,10},{10,12},{12,14},{14,0},{1,3},{3,5},... | collective-permute-start | bytes 1572872 | tf_op jit(solution)/shard_map/ppermute | solution.py:16
  326.1 20.6 %collective-permute-start.9 = (bf16[128,2048]{1,0:T(8,128)(2,1)S(1)}, bf16[128,2048]{1,0:T(8,128)(2,1)S(1)}, u32[]{:S(2)}, u32[]{:S(2)}) collective-permute-start(bf16[128,2048]{1,0:T(8,128)(2,1)S(1)} %collective-permute-done.8), channel_id=1, source_target_pairs={{0,2},{2,4},{4,6},{6,8},{8,10},{10,12},{12,14},{14,0},{1,3},{3,5},... | collective-permute-start | bytes 1572872 | tf_op jit(solution)/shard_map/ppermute | solution.py:16
  326.1 23.6 %collective-permute-start.12 = (bf16[128,2048]{1,0:T(8,128)(2,1)S(1)}, bf16[128,2048]{1,0:T(8,128)(2,1)S(1)}, u32[]{:S(2)}, u32[]{:S(2)}) collective-permute-start(bf16[128,2048]{1,0:T(8,128)(2,1)S(1)} %fusion.59), channel_id=1, source_target_pairs={{0,14},{2,0},{4,2},{6,4},{8,6},{10,8},{12,10},{14,12},{1,15},{3,1}... | collective-permute-start | bytes 1572872 | tf_op jit(solution)/shard_map/ppermute | solution.py:18
  346.7 24.0 %collective-permute-start.10 = (bf16[128,2048]{1,0:T(8,128)(2,1)S(1)}, bf16[128,2048]{1,0:T(8,128)(2,1)S(1)}, u32[]{:S(2)}, u32[]{:S(2)}) collective-permute-start(bf16[128,2048]{1,0:T(8,128)(2,1)S(1)} %collective-permute-done.9), channel_id=1, source_target_pairs={{0,2},{2,4},{4,6},{6,8},{8,10},{10,12},{12,14},{14,0},{1,3},{3,5},... | collective-permute-start | bytes 1572872 | tf_op jit(solution)/shard_map/ppermute | solution.py:16
  349.8 23.7 %collective-permute-start.13 = (bf16[128,2048]{1,0:T(8,128)(2,1)S(1)}, bf16[128,2048]{1,0:T(8,128)(2,1)S(1)}, u32[]{:S(2)}, u32[]{:S(2)}) collective-permute-start(bf16[128,2048]{1,0:T(8,128)(2,1)S(1)} %collective-permute-done.12), channel_id=1, source_target_pairs={{0,14},{2,0},{4,2},{6,4},{8,6},{10,8},{12,10},{14,12},{1,15},{3,1}... | collective-permute-start | bytes 1572872 | tf_op jit(solution)/shard_map/ppermute | solution.py:18
  370.7 23.8 %collective-permute-start.11 = (bf16[128,2048]{1,0:T(8,128)(2,1)S(1)}, bf16[128,2048]{1,0:T(8,128)(2,1)S(1)}, u32[]{:S(2)}, u32[]{:S(2)}) collective-permute-start(bf16[128,2048]{1,0:T(8,128)(2,1)S(1)} %collective-permute-done.10), channel_id=1, source_target_pairs={{0,2},{2,4},{4,6},{6,8},{8,10},{10,12},{12,14},{14,0},{1,3},{3,5},... | collective-permute-start | bytes 1572872 | tf_op jit(solution)/shard_map/ppermute | solution.py:16
  373.5 24.2 %collective-permute-start.14 = (bf16[128,2048]{1,0:T(8,128)(2,1)S(1)}, bf16[128,2048]{1,0:T(8,128)(2,1)S(1)}, u32[]{:S(2)}, u32[]{:S(2)}) collective-permute-start(bf16[128,2048]{1,0:T(8,128)(2,1)S(1)} %collective-permute-done.13), channel_id=1, source_target_pairs={{0,14},{2,0},{4,2},{6,4},{8,6},{10,8},{12,10},{14,12},{1,15},{3,1}... | collective-permute-start | bytes 1572872 | tf_op jit(solution)/shard_map/ppermute | solution.py:18
  397.8 5.7 copy-start.27
  403.5 14.4 %copy-start.1 = (f32[128,8,2,512]{3,1,2,0:T(8,128)S(1)}, f32[128,8,2,512]{3,1,2,0:T(8,128)}, u32[]{:S(2)}) copy-start(f32[128,8,2,512]{3,1,2,0:T(8,128)} %copy-done) | copy-start | bytes 12582916
  403.5 14.4 %copy-start.8 = (bf16[1024,2048]{1,0:T(8,128)(2,1)S(1)}, bf16[1024,2048]{1,0:T(8,128)(2,1)}, u32[]{:S(2)}) copy-start(bf16[1024,2048]{1,0:T(8,128)(2,1)} %get-tuple-element.117) | copy-start | bytes 12582916
  428.9 125.6 %copy-start.15 = (bf16[1024,1024]{1,0:T(8,128)(2,1)}, bf16[1024,1024]{1,0:T(8,128)(2,1)S(1)}, u32[]{:S(2)}) copy-start(bf16[1024,1024]{1,0:T(8,128)(2,1)S(1)} %get-tuple-element.112) | copy-start | bytes 6291460
  443.6 92.8 %copy-start.17 = (bf16[8,16,2048]{2,1,0:T(8,128)(2,1)S(1)}, bf16[8,16,2048]{2,1,0:T(8,128)(2,1)}, u32[]{:S(2)}) copy-start(bf16[8,16,2048]{2,1,0:T(8,128)(2,1)} %param.19) | copy-start | bytes 1572868
  443.6 265.6 %reduce-scatter.7.cloned.1.call-start = ((), (), s32[]{:S(2)}) async-start(), calls=%async_computation.6 | async-start | bytes 4718592 | tf_op jit(solution)/shard_map/reduce_scatter | solution.py:82
  537.8 15.2 %copy-start.25 = (bf16[128,2048]{1,0:T(8,128)(2,1)}, bf16[128,2048]{1,0:T(8,128)(2,1)S(1)}, u32[]{:S(2)}) copy-start(bf16[128,2048]{1,0:T(8,128)(2,1)S(1)} %fusion.64) | copy-start | bytes 1572868
  537.8 15.2 %collective-permute-start.22 = (bf16[128,2048]{1,0:T(8,128)(2,1)S(1)}, bf16[128,2048]{1,0:T(8,128)(2,1)S(1)}, u32[]{:S(2)}, u32[]{:S(2)}) collective-permute-start(bf16[128,2048]{1,0:T(8,128)(2,1)S(1)} %fusion.64), channel_id=1, source_target_pairs={{16,0},{17,1},{18,2},{19,3},{20,4},{21,5},{22,6},{23,7},{24,8},{25... | collective-permute-start | bytes 1572872 | tf_op jit(solution)/shard_map/ppermute | solution.py:26
  553.0 101.6 %copy-start.18 = (bf16[128,2048]{1,0:T(8,128)(2,1)}, bf16[128,2048]{1,0:T(8,128)(2,1)S(1)}, u32[]{:S(2)}) copy-start(bf16[128,2048]{1,0:T(8,128)(2,1)S(1)} %collective-permute-done.22) | copy-start | bytes 1572868
  553.0 15.2 %collective-permute-start.23 = (bf16[128,2048]{1,0:T(8,128)(2,1)S(1)}, bf16[128,2048]{1,0:T(8,128)(2,1)}, u32[]{:S(2)}, u32[]{:S(2)}) collective-permute-start(bf16[128,2048]{1,0:T(8,128)(2,1)S(1)} %collective-permute-done.22), channel_id=1, source_target_pairs={{0,2},{2,4},{4,6},{6,8},{8,10},{10,12},{12,14},{14,0},{1,3},{3,5},... | collective-permute-start | bytes 1572872 | tf_op jit(solution)/shard_map/ppermute | solution.py:16
  562.8 219.2 %reduce-scatter.11.cloned.1.call-start = ((), (), s32[]{:S(2)}) async-start(), calls=%async_computation.8 | async-start | bytes 4718592 | tf_op jit(solution)/shard_map/reduce_scatter | solution.py:82
  568.2 26.5 %collective-permute-start.24 = (bf16[128,2048]{1,0:T(8,128)(2,1)}, bf16[128,2048]{1,0:T(8,128)(2,1)S(1)}, u32[]{:S(2)}, u32[]{:S(2)}) collective-permute-start(bf16[128,2048]{1,0:T(8,128)(2,1)} %collective-permute-done.23), channel_id=1, source_target_pairs={{0,2},{2,4},{4,6},{6,8},{8,10},{10,12},{12,14},{14,0},{1,3},{3,5},... | collective-permute-start | bytes 1572872 | tf_op jit(solution)/shard_map/ppermute | solution.py:16
  568.2 28.9 %collective-permute-start.27 = (bf16[128,2048]{1,0:T(8,128)(2,1)S(1)}, bf16[128,2048]{1,0:T(8,128)(2,1)S(1)}, u32[]{:S(2)}, u32[]{:S(2)}) collective-permute-start(bf16[128,2048]{1,0:T(8,128)(2,1)S(1)} %collective-permute-done.22), channel_id=1, source_target_pairs={{0,14},{2,0},{4,2},{6,4},{8,6},{10,8},{12,10},{14,12},{1,15},{3,1}... | collective-permute-start | bytes 1572872 | tf_op jit(solution)/shard_map/ppermute | solution.py:18
  594.7 29.1 %collective-permute-start.25 = (bf16[128,2048]{1,0:T(8,128)(2,1)S(1)}, bf16[128,2048]{1,0:T(8,128)(2,1)S(1)}, u32[]{:S(2)}, u32[]{:S(2)}) collective-permute-start(bf16[128,2048]{1,0:T(8,128)(2,1)S(1)} %collective-permute-done.24), channel_id=1, source_target_pairs={{0,2},{2,4},{4,6},{6,8},{8,10},{10,12},{12,14},{14,0},{1,3},{3,5},... | collective-permute-start | bytes 1572872 | tf_op jit(solution)/shard_map/ppermute | solution.py:16
  597.1 29.2 %collective-permute-start.28 = (bf16[128,2048]{1,0:T(8,128)(2,1)S(1)}, bf16[128,2048]{1,0:T(8,128)(2,1)S(1)}, u32[]{:S(2)}, u32[]{:S(2)}) collective-permute-start(bf16[128,2048]{1,0:T(8,128)(2,1)S(1)} %collective-permute-done.27), channel_id=1, source_target_pairs={{0,14},{2,0},{4,2},{6,4},{8,6},{10,8},{12,10},{14,12},{1,15},{3,1}... | collective-permute-start | bytes 1572872 | tf_op jit(solution)/shard_map/ppermute | solution.py:18
  623.8 29.5 %collective-permute-start.26 = (bf16[128,2048]{1,0:T(8,128)(2,1)S(1)}, bf16[128,2048]{1,0:T(8,128)(2,1)S(1)}, u32[]{:S(2)}, u32[]{:S(2)}) collective-permute-start(bf16[128,2048]{1,0:T(8,128)(2,1)S(1)} %collective-permute-done.25), channel_id=1, source_target_pairs={{0,2},{2,4},{4,6},{6,8},{8,10},{10,12},{12,14},{14,0},{1,3},{3,5},... | collective-permute-start | bytes 1572872 | tf_op jit(solution)/shard_map/ppermute | solution.py:16
  626.3 28.6 %collective-permute-start.29 = (bf16[128,2048]{1,0:T(8,128)(2,1)S(1)}, bf16[128,2048]{1,0:T(8,128)(2,1)S(1)}, u32[]{:S(2)}, u32[]{:S(2)}) collective-permute-start(bf16[128,2048]{1,0:T(8,128)(2,1)S(1)} %collective-permute-done.28), channel_id=1, source_target_pairs={{0,14},{2,0},{4,2},{6,4},{8,6},{10,8},{12,10},{14,12},{1,15},{3,1}... | collective-permute-start | bytes 1572872 | tf_op jit(solution)/shard_map/ppermute | solution.py:18
  655.0 4.7 copy-start.2
  655.0 4.7 copy-start.12
  659.7 10.1 %copy-start.10 = (bf16[1024,2048]{1,0:T(8,128)(2,1)}, bf16[1024,2048]{1,0:T(8,128)(2,1)S(1)}, u32[]{:S(2)}) copy-start(bf16[1024,2048]{1,0:T(8,128)(2,1)S(1)} %fusion.52) | copy-start | bytes 12582916
  659.7 12.1 %copy-start.28 = (bf16[2048,512]{1,0:T(8,128)(2,1)S(1)}, bf16[2048,512]{1,0:T(8,128)(2,1)}, u32[]{:S(2)}) copy-start(bf16[2048,512]{1,0:T(8,128)(2,1)} %get-tuple-element.115) | copy-start | bytes 6291460
  692.5 10.1 %copy-start.7 = (bf16[1024,1024]{1,0:T(8,128)(2,1)S(1)}, bf16[1024,1024]{1,0:T(8,128)(2,1)}, u32[]{:S(2)}) copy-start(bf16[1024,1024]{1,0:T(8,128)(2,1)} %copy-done.6) | copy-start | bytes 6291460
  702.5 31.7 %collective-permute-start.30 = (bf16[1024,2048]{1,0:T(8,128)(2,1)}, bf16[1024,2048]{1,0:T(8,128)(2,1)}, u32[]{:S(2)}, u32[]{:S(2)}) collective-permute-start(bf16[1024,2048]{1,0:T(8,128)(2,1)} %get-tuple-element.122), channel_id=1, source_target_pairs={{0,1},{1,0},{2,3},{3,2},{4,5},{5,4},{6,7},{7,6},{8,9},{9,8},{10,11... | collective-permute-start | bytes 12582920 | tf_op jit(solution)/shard_map/ppermute | solution.py:234
  702.6 6.6 copy-start.14
  708.7 20.4 %collective-permute-start.31 = (bf16[512,2048]{1,0:T(8,128)(2,1)}, bf16[512,2048]{1,0:T(8,128)(2,1)}, u32[]{:S(2)}, u32[]{:S(2)}) collective-permute-start(bf16[512,2048]{1,0:T(8,128)(2,1)} %get-tuple-element.124), channel_id=1, source_target_pairs={{0,1},{1,0},{2,3},{3,2},{4,5},{5,4},{6,7},{7,6},{8,9},{9,8},{10,11... | collective-permute-start | bytes 6291464 | tf_op jit(solution)/shard_map/ppermute | solution.py:234
  729.1 6.2 copy-start.5
  739.4 42.6 %copy-start.4 = (bf16[8,16,2048]{2,1,0:T(8,128)(2,1)S(1)}, bf16[8,16,2048]{2,1,0:T(8,128)(2,1)}, u32[]{:S(2)}) copy-start(bf16[8,16,2048]{2,1,0:T(8,128)(2,1)} %param.18) | copy-start | bytes 1572868
  739.5 42.6 %copy-start.33 = (f32[128]{0:T(128)S(1)}, f32[128]{0:T(128)}, u32[]{:S(2)}) copy-start(f32[128]{0:T(128)} %copy-done.32) | copy-start | bytes 1540
  739.5 43.9 %copy-start.19 = (bf16[128,2048]{1,0:T(8,128)(2,1)S(1)}, bf16[128,2048]{1,0:T(8,128)(2,1)}, u32[]{:S(2)}) copy-start(bf16[128,2048]{1,0:T(8,128)(2,1)} %copy-done.18) | copy-start | bytes 1572868
  739.5 43.9 %copy-start.26 = (bf16[128,2048]{1,0:T(8,128)(2,1)S(1)}, bf16[128,2048]{1,0:T(8,128)(2,1)}, u32[]{:S(2)}) copy-start(bf16[128,2048]{1,0:T(8,128)(2,1)} %copy-done.25) | copy-start | bytes 1572868
  (8 other events, 20.0 us)
Sparse Core Ops, SparseCore 0:
  204.7 90.3 reduce-scatter.4
  443.7 91.1 reduce-scatter.8
  562.9 127.6 reduce-scatter.6
  694.0 87.9 reduce-scatter.10
